TPU v7x, 32 devices: a whole 2x2x4 slice. The times are simulated.
32 devices in a mesh: seq: 8 (over z, x), tp: 4 (over y, core).
Axes of the slice: x: 2, y: 2, z: 4, core: 2. Of those that a mesh axis runs over, the one named last changes fastest.
Arguments:
- queries: bfloat16 [4096, 4096], P('seq', 'tp'), may hold values from -6 to 6
- keys: bfloat16 [4096, 4096], P('seq', 'tp'), may hold values from -6 to 6
- values: bfloat16 [4096, 4096], P('seq', 'tp'), may hold values from -6 to 6
- log_decay: float32 [4096, 32], P('seq', 'tp'), may hold values from -1.2 to 0, as said below
- out_weight: bfloat16 [4096, 6144], P('tp', 'seq'), may hold values from -0.09375 to 0.09375
- grad_out: bfloat16 [4096, 6144], P('seq', 'tp'), may hold values from -6 to 6
Outputs:
- grad_queries: bfloat16 [4096, 4096], P('seq', 'tp')
- grad_keys: bfloat16 [4096, 4096], P('seq', 'tp')
- grad_values: bfloat16 [4096, 4096], P('seq', 'tp')
- grad_weight: float32 [6144, 4096], P('seq', 'tp')
Inputs may be any that keep to these rules, and one draw needn't show every extreme that they name: `log_decay`: log decay of each head's state at each token.
All inputs are finite; a program needn't handle non-finite values.
Results may differ from a plain program's by a relative error of at most 0.0029.
Values may be sent and summed in bfloat16 or wider, within the bound.
A program may use at most 192 MiB of HBM per device.

v0:
```python
import jax
import jax.numpy as jnp
from jax import lax
from jax.sharding import PartitionSpec as P

BLOCK = 256
EPS = 1e-06
HIGH = lax.Precision.HIGHEST


def carried_in(value, axis, join, neutral, backward):
    count, mine = (lax.axis_size(axis), lax.axis_index(axis))
    pieces = jax.tree.map(lambda part: lax.all_gather(part, axis), value)
    if backward:
        pieces = jax.tree.map(lambda part: part[::-1], pieces)
        mine = count - 1 - mine
    total = jax.tree.map(
        lambda part, zero: jnp.full_like(part, 0) + jnp.asarray(zero, part.dtype), value, neutral
    )

    def turn(position, total):
        longer = join(total, jax.tree.map(lambda part: part[position], pieces))
        return jax.tree.map(lambda new, old: jnp.where(position < mine, new, old), longer, total)

    return lax.fori_loop(0, count - 1, turn, total)


def chain(earlier, later):
    log_early, state_early = earlier
    log_late, state_late = later
    return (log_early + log_late, jnp.exp(log_late)[:, None, None] * state_early + state_late)


def on_device(queries, keys, values, log_decay, out_weight, grad_out):
    tok_rows = queries.shape[0]
    heads_here = log_decay.shape[1]
    head_size = queries.shape[1] // heads_here
    blocks = tok_rows // BLOCK
    shape4 = (blocks, BLOCK, heads_here, head_size)
    query_b = queries.reshape(shape4)
    key_b = keys.reshape(shape4)
    query_f = queries.astype(jnp.float32).reshape(shape4)
    key_f = keys.astype(jnp.float32).reshape(shape4)
    value_f = values.astype(jnp.float32).reshape(shape4)
    rates = log_decay.reshape(blocks, BLOCK, heads_here)
    cumul = jnp.cumsum(rates, axis=1)
    totals = cumul[:, -1, :]
    running = jnp.cumsum(totals, axis=0)
    before = running - totals
    dev_log = running[-1]
    cumul_t = jnp.transpose(cumul, (0, 2, 1))
    lower = jnp.arange(BLOCK)[:, None] >= jnp.arange(BLOCK)[None, :]
    decay_mat = jnp.where(
        lower[None, None],
        jnp.exp(jnp.minimum(cumul_t[:, :, :, None] - cumul_t[:, :, None, :], 0.0)),
        0.0,
    )
    scores = (
        jnp.einsum("nthd,nshd->nhts", query_b, key_b, preferred_element_type=jnp.float32)
        * decay_mat
    )
    into_end = jnp.exp(totals[:, None, :] - cumul)
    from_start = jnp.exp(cumul)
    block_states = jnp.einsum("nth,nthd,nthe->nhde", into_end, key_f, value_f, precision=HIGH)
    order = jnp.arange(blocks)
    earlier_mask = order[None, :] < order[:, None]
    forward_mix = jnp.where(
        earlier_mask[:, :, None],
        jnp.exp(jnp.minimum(before[:, None, :] - running[None, :, :], 0.0)),
        0.0,
    )
    prefix_local = jnp.einsum("nmh,mhde->nhde", forward_mix, block_states, precision=HIGH)
    dev_state = jnp.einsum(
        "mh,mhde->hde", jnp.exp(dev_log[None, :] - running), block_states, precision=HIGH
    )
    zero_log = jnp.zeros_like(dev_log)
    zero_state = jnp.zeros_like(dev_state)
    state_in = carried_in((dev_log, dev_state), "seq", chain, (zero_log, zero_state), False)[1]
    start_states = prefix_local + jnp.exp(before)[:, :, None, None] * state_in[None]
    attended = jnp.einsum("nhts,nshd->nthd", scores, value_f, precision=HIGH)
    attended = attended + from_start[..., None] * jnp.einsum(
        "nthd,nhde->nthe", query_f, start_states, precision=HIGH
    )
    scale = jnp.sqrt(jnp.mean(attended * attended, axis=-1, keepdims=True) + EPS)
    o_hat = attended / scale
    normed = o_hat.reshape(tok_rows, -1).astype(jnp.bfloat16)
    cotangent = lax.all_gather(grad_out, "tp", axis=1, tiled=True)
    grad_normed = lax.dot_general(
        cotangent,
        lax.all_gather(out_weight, "seq", axis=1, tiled=True),
        (((1,), (1,)), ((), ())),
        preferred_element_type=jnp.float32,
    )
    grad_hat = grad_normed.reshape(shape4)
    grad_att = (grad_hat - o_hat * jnp.mean(grad_hat * o_hat, axis=-1, keepdims=True)) / scale
    grad_mix = jnp.einsum("nthe,nshe->nhts", grad_att, value_f, precision=HIGH) * decay_mat
    grad_q = jnp.einsum("nhts,nshd->nthd", grad_mix, key_f, precision=HIGH)
    grad_q = grad_q + from_start[..., None] * jnp.einsum(
        "nthe,nhde->nthd", grad_att, start_states, precision=HIGH
    )
    block_grads = jnp.einsum("nth,nthd,nthe->nhde", from_start, query_f, grad_att, precision=HIGH)
    later_mask = order[None, :] > order[:, None]
    backward_mix = jnp.where(
        later_mask[:, :, None],
        jnp.exp(jnp.minimum(before[None, :, :] - running[:, None, :], 0.0)),
        0.0,
    )
    suffix_local = jnp.einsum("nmh,mhde->nhde", backward_mix, block_grads, precision=HIGH)
    dev_grad = jnp.einsum("mh,mhde->hde", jnp.exp(before), block_grads, precision=HIGH)
    grad_in = carried_in((dev_log, dev_grad), "seq", chain, (zero_log, zero_state), True)[1]
    end_grads = suffix_local + jnp.exp(dev_log[None, :] - running)[:, :, None, None] * grad_in[None]
    grad_k = jnp.einsum("nhts,nthd->nshd", grad_mix, query_f, precision=HIGH)
    grad_k = grad_k + into_end[..., None] * jnp.einsum(
        "nthe,nhde->nthd", value_f, end_grads, precision=HIGH
    )
    grad_v = jnp.einsum("nhts,nthe->nshe", scores, grad_att, precision=HIGH)
    grad_v = grad_v + into_end[..., None] * jnp.einsum(
        "nthd,nhde->nthe", key_f, end_grads, precision=HIGH
    )
    by_columns = lax.all_to_all(cotangent, "seq", split_axis=1, concat_axis=0, tiled=True)
    grad_weight = lax.dot_general(
        by_columns,
        lax.all_gather(normed, "seq", axis=0, tiled=True),
        (((0,), (0,)), ((), ())),
        preferred_element_type=jnp.float32,
    )
    return (
        grad_q.reshape(tok_rows, -1).astype(jnp.bfloat16),
        grad_k.reshape(tok_rows, -1).astype(jnp.bfloat16),
        grad_v.reshape(tok_rows, -1).astype(jnp.bfloat16),
        grad_weight,
    )


def solution(mesh):
    placed = (
        P("seq", "tp"),
        P("seq", "tp"),
        P("seq", "tp"),
        P("seq", "tp"),
        P("tp", "seq"),
        P("seq", "tp"),
    )
    return jax.shard_map(
        on_device,
        mesh=mesh,
        in_specs=placed,
        out_specs=(P("seq", "tp"), P("seq", "tp"), P("seq", "tp"), P("seq", "tp")),
        check_vma=False,
    )
```

profile of v0, /device:TPU:0, one launch (start us, length us, event | category | flops | bytes accessed | tf_op | source)
XLA Modules:
  0.0 677.9 jit_solution(5137441906326079839)
XLA Ops:
  13.5 2.8 fusion.22
  17.3 4.4 fusion.47
  27.6 22.4 %all-gather.2 = f32[8,1,8]{2,1,0:T(1,128)S(1)} all-gather(f32[1,1,8]{2,1,0:T(1,128)S(1)} %get-tuple-element.278), channel_id=1, replica_groups=mesh['seq'=8,'tp'=4] {'seq'}, dimensions={0}, use_global_device_ids=true | all-gather | bytes 288 | tf_op jit(solution)/shard_map/all_gather | solution.py:13
  50.0 6.3 fusion.49
  60.4 5.0 fusion.6
  65.4 32.6 %all-gather.15.cloned.1.call-done = f32[64,128,128]{2,1,0:T(8,128)} async-done(((f32[8,128,128]{2,1,0:T(8,128)}), f32[64,128,128]{2,1,0:T(8,128)}) %all-gather.15.cloned.1.call-update) | async-done | bytes 4194320 | tf_op jit(solution)/shard_map/all_gather | solution.py:13
  98.0 8.7 %while.28 = (s32[]{:T(128)}, f32[8,128,128]{2,1,0:T(8,128)S(1)}, s32[]{:T(128)}, f32[8,8]{1,0:T(8,128)S(1)}, f32[8,8,128,128]{3,2,1,0:T(8,128)}, /*index=5*/s32[]{:T(128)}, s32[]{:T(128)}) while((s32[]{:T(128)}, f32[8,128,128]{2,1,0:T(8,128)S(1)}, s32[]{:T(128)}, f32[8,8]{1,0:T(8,128)S(1)}, f32[8,8,128,128]{3,2,1,0:T(8,128)}, ...), condition=%wide.region_4.5_spmd.clone, body=%wide.region_3.4_spmd.clone.sunk | while | flops 524292 | bytes 1573073 | solution.py:25
  106.7 4.5 multiply_reduce_fusion.1
  111.2 33.0 %all-gather.9.cloned.1.call-done = bf16[512,6144]{0,1:T(8,128)(2,1)} async-done(((bf16[512,1536]{0,1:T(8,128)(2,1)}), bf16[512,6144]{0,1:T(8,128)(2,1)}) %all-gather.9.cloned.1.call-update) | async-done | bytes 6291472 | tf_op jit(solution)/shard_map/all_gather | solution.py:87
  144.2 178.5 %all-gather.11.cloned.1.call-done = bf16[1024,6144]{1,0:T(8,128)(2,1)} async-done(((bf16[1024,768]{1,0:T(8,128)(2,1)}), bf16[1024,6144]{1,0:T(8,128)(2,1)}) %all-gather.11.cloned.1.call-update) | async-done | bytes 12582928 | tf_op jit(solution)/shard_map/all_gather | solution.py:90
  322.7 11.5 %convolution_bitcast_fusion.1 = f32[64,8,8,128]{3,1,2,0:T(8,128)S(1)} fusion(bf16[512,6144]{0,1:T(8,128)(2,1)} %all-gather.9.cloned.1.call-done, bf16[1024,6144]{1,0:T(8,128)(2,1)} %all-gather.11.cloned.1.call-done), kind=kOutput, calls=%fused_computation.50 | convolution fusion | flops 6442450944 | bytes 20971520 | tf_op jit(solution)/shard_map/dot_general | solution.py:88
  336.0 2.9 copy.187
  341.2 3.1 fusion.93
  347.5 4.6 fusion.43
  352.2 4.8 all-to-all-start
  357.0 2.5 copy.210
  359.5 2.5 copy.277
  362.1 193.0 %all-to-all-done = bf16[512,8,768]{0,2,1:T(8,128)(2,1)} async-done(((bf16[512,8,768]{0,2,1:T(8,128)(2,1)}), bf16[512,8,768]{0,2,1:T(8,128)(2,1)}, u32[]{:S(2)}, u32[]{:S(2)}) %all-to-all-start) | async-done | bytes 6291488 | tf_op jit(solution)/shard_map/all_to_all | solution.py:120
  555.1 8.6 %copy.211 = bf16[8,512,768]{2,1,0:T(8,128)(2,1)} copy(bf16[8,512,768]{1,2,0:T(8,128)(2,1)} %bitcast.34) | data formatting | bytes 12582912 | tf_op jit(solution)/shard_map/all_to_all | solution.py:120
  563.7 3.2 fusion.53
  567.0 3.7 fusion.10
  570.7 3.2 fusion.17
  573.9 2.8 copy.193
  576.7 2.6 copy.278
  579.2 6.3 fusion.45
  585.6 8.0 %fusion.8 = f32[2,8,256,128]{3,2,1,0:T(8,128)} fusion(bf16[2,256,8,128]{1,3,2,0:T(8,128)(2,1)S(1)} %copy-done.6, f32[2,8,256,256]{3,2,1,0:T(8,128)} %copy-done.13, f32[2,8,256]{2,1,0:T(8,128)S(1)} %add_bitcast_fusion.1, pred[256,256]{1,0:T(8,128)(4,1)S(1)} %iota_compare_fusion), kind=kOutput, calls=%fused_computation.11 | convolution fusion | flops 1614807040 | bytes 7421952 | tf_op jit(solution)/shard_map/nhts,nthd->nshd/dot_general | solution.py:112
  593.6 9.2 %fusion.4 = f32[2,8,128,256]{2,3,1,0:T(8,128)} fusion(f32[2,256,8,128]{1,3,2,0:T(8,128)S(1)} %get-tuple-element.275, f32[2,8,256,256]{3,2,1,0:T(8,128)S(1)} %copy-done.3, f32[2,8,256]{2,1,0:T(8,128)S(1)} %add_bitcast_fusion.1, pred[256,256]{1,0:T(8,128)(4,1)S(1)} %iota_compare_fusion), kind=kOutput, calls=%fused_computation.9 | convolution fusion | flops 1614807040 | bytes 8470528 | tf_op jit(solution)/shard_map/nhts,nthe->nshe/dot_general | solution.py:116
  602.8 4.7 rev.7
  607.5 8.6 %while.29 = (s32[]{:T(128)}, f32[8,128,128]{2,1,0:T(8,128)S(1)}, s32[]{:T(128)}, f32[8,8]{1,0:T(8,128)S(1)}, f32[8,8,128,128]{3,2,1,0:T(8,128)}, /*index=5*/s32[]{:T(128)}, s32[]{:T(128)}) while((s32[]{:T(128)}, f32[8,128,128]{2,1,0:T(8,128)S(1)}, s32[]{:T(128)}, f32[8,8]{1,0:T(8,128)S(1)}, f32[8,8,128,128]{3,2,1,0:T(8,128)}, ...), condition=%wide.region_8.9_spmd.clone, body=%wide.region_7.8_spmd.clone.sunk | while | flops 524292 | bytes 1573073 | solution.py:25
  616.1 3.4 fusion.13
  624.5 33.3 %all-gather.13.cloned.1.call-done = bf16[4096,1024]{1,0:T(8,128)(2,1)} async-done(((bf16[512,1024]{1,0:T(8,128)(2,1)}), bf16[4096,1024]{1,0:T(8,128)(2,1)}) %all-gather.13.cloned.1.call-update) | async-done | bytes 8388624 | tf_op jit(solution)/shard_map/all_gather | solution.py:123
  657.8 11.0 %convolution_bitcast_fusion = f32[768,1024]{0,1:T(8,128)S(1)} fusion(bf16[4096,1024]{1,0:T(8,128)(2,1)} %all-gather.13.cloned.1.call-done, bf16[4096,768]{1,0:T(8,128)(2,1)} %bitcast.156), kind=kOutput, calls=%fused_computation.49 | convolution fusion | flops 6442450944 | bytes 17825792 | tf_op jit(solution)/shard_map/dot_general | solution.py:121
  (118 shorter events, 48.7 us)
Async XLA Ops:
  7.2 90.8 %all-gather.15.cloned.1.call-start = ((), (), s32[]{:S(2)}) async-start(), calls=%async_computation.4 | async-start | bytes 4718592 | tf_op jit(solution)/shard_map/all_gather | solution.py:13
  11.6 1.9 copy-start.10
  13.5 44.8 %copy-start.8 = (bf16[64,8,8,128]{3,2,1,0:T(8,128)(2,1)}, bf16[64,8,8,128]{3,2,1,0:T(8,128)(2,1)S(1)}, u32[]{:S(2)}) copy-start(bf16[64,8,8,128]{3,2,1,0:T(8,128)(2,1)S(1)} %copy.234) | copy-start | bytes 3145732
  13.5 8.3 %copy-start.16 = (bf16[512,1536]{1,0:T(8,128)(2,1)S(1)}, bf16[512,1536]{1,0:T(8,128)(2,1)}, u32[]{:S(2)}) copy-start(bf16[512,1536]{1,0:T(8,128)(2,1)} %param.15) | copy-start | bytes 4718596
  16.3 1.0 copy-start.17
  21.7 122.5 %all-gather.9.cloned.1.call-start = ((), (), s32[]{:S(2)}) async-start(), calls=%async_computation.1 | async-start | bytes 7864320 | tf_op jit(solution)/shard_map/all_gather | solution.py:87
  23.4 1.3 copy-start.18
  23.4 299.3 %all-gather.11.cloned.1.call-start = ((), (), s32[]{:S(2)}) async-start(), calls=%async_computation.2 | async-start | bytes 14155776 | tf_op jit(solution)/shard_map/all_gather | solution.py:90
  24.1 578.6 %all-gather.17.cloned.1.call-start = ((), (), s32[]{:S(2)}) async-start(), calls=%async_computation.5 | async-start | bytes 4718592 | tf_op jit(solution)/shard_map/all_gather | solution.py:13
  27.5 30.8 %copy-start.4 = (bf16[2,256,8,128]{1,3,2,0:T(8,128)(2,1)}, bf16[2,256,8,128]{1,3,2,0:T(8,128)(2,1)S(1)}, u32[]{:S(2)}) copy-start(bf16[2,256,8,128]{1,3,2,0:T(8,128)(2,1)S(1)} %copy.196) | copy-start | bytes 3145732
  58.3 2.0 copy-start.2
  111.2 227.7 %copy-start = (f32[2,256,8,128]{1,3,2,0:T(8,128)}, f32[2,256,8,128]{1,3,2,0:T(8,128)S(1)}, u32[]{:S(2)}) copy-start(f32[2,256,8,128]{1,3,2,0:T(8,128)S(1)} %get-tuple-element.280) | copy-start | bytes 6291460
  338.9 2.2 copy-start.1
  341.1 3.1 copy-start.5
  346.5 1.0 copy-start.14
  352.2 202.9 %all-to-all-start = ((bf16[512,8,768]{0,2,1:T(8,128)(2,1)}), bf16[512,8,768]{0,2,1:T(8,128)(2,1)}, u32[]{:S(2)}, u32[]{:S(2)}) async-start(bf16[512,8,768]{0,2,1:T(8,128)(2,1)} %bitcast.155), calls=%async_computation | async-start | bytes 12582912 | tf_op jit(solution)/shard_map/all_to_all | solution.py:120
  357.0 300.8 %all-gather.13.cloned.1.call-start = ((), (), s32[]{:S(2)}) async-start(), calls=%async_computation.3 | async-start | bytes 9437184 | tf_op jit(solution)/shard_map/all_gather | solution.py:123
  563.7 3.2 copy-start.11
  566.9 3.7 copy-start.13
  566.9 3.7 copy-start.12
  576.7 8.9 %copy-start.6 = (bf16[2,256,8,128]{1,3,2,0:T(8,128)(2,1)S(1)}, bf16[2,256,8,128]{1,3,2,0:T(8,128)(2,1)}, u32[]{:S(2)}) copy-start(bf16[2,256,8,128]{1,3,2,0:T(8,128)(2,1)} %copy-done.4) | copy-start | bytes 3145732
  585.5 8.0 %copy-start.3 = (f32[2,8,256,256]{3,2,1,0:T(8,128)S(1)}, f32[2,8,256,256]{3,2,1,0:T(8,128)}, u32[]{:S(2)}) copy-start(f32[2,8,256,256]{3,2,1,0:T(8,128)} %copy-done.2) | copy-start | bytes 12582916
  607.5 8.6 %copy-start.7 = (f32[8,128,128,2]{2,3,1,0:T(2,128)S(1)}, f32[8,128,128,2]{2,3,1,0:T(2,128)}, u32[]{:S(2)}) copy-start(f32[8,128,128,2]{2,3,1,0:T(2,128)} %fusion.45) | copy-start | bytes 3145732
  616.1 4.1 copy-start.9
  616.1 4.1 copy-start.15
Sparse Core Ops, SparseCore 0:
  21.8 76.1 all-gather.14
  99.6 44.6 all-gather.8
  146.5 176.2 all-gather.10
  352.3 177.9 all-gather.16
  532.3 125.4 all-gather.12
where the time goes:
time: 687 us; the launch traced here: 678 us
  waiting for transfers between devices  471 us (69%)
  matrix products  93.1 us (14%)
  local copies, waits for them, and re-layouts  46.9 us (7%)
  other arithmetic  24.7 us (4%)
  blocking collectives  22.4 us (3%)
  between operations  14.4 us (2%)
    all_to_all x1, waiting for transfers between devices, on_device(): lax.all_to_all(cotangent, 'seq', split_axis=1, concat_axis=0, tiled=True)  193 us
    all_gather x1, waiting for transfers between devices, on_device(): lax.all_gather(out_weight, 'seq', axis=1, tiled=True)  178 us
    all_gather x1, waiting for transfers between devices, on_device(): lax.all_gather(normed, 'seq', axis=0, tiled=True)  33.3 us
    all_gather x1, waiting for transfers between devices, on_device(): cotangent = lax.all_gather(grad_out, 'tp', axis=1, tiled=True)  33 us
    all_gather x2, waiting for transfers between devices, carried_in(): pieces = jax.tree.map(lambda part: lax.all_gather(part, axis), value)  32.6 us
    all_gather x1, blocking collectives, carried_in(): pieces = jax.tree.map(lambda part: lax.all_gather(part, axis), value)  22.4 us
    unnamed x46, local copies, waits for them, and re-layouts  19.6 us
    select_n x14, other arithmetic, turn(): jnp.where(position < mine, new, old)  16.8 us
  transfers between devices with their start and end apart: 6, of which 5 were waited for; matrix products, arithmetic and copies ran while one was open for 16% of the time, Pallas kernels for 0%

commit v1 on v0

--- a/solution.py
+++ b/solution.py
@@ -84,7 +84,14 @@
     scale = jnp.sqrt(jnp.mean(attended * attended, axis=-1, keepdims=True) + EPS)
     o_hat = attended / scale
     normed = o_hat.reshape(tok_rows, -1).astype(jnp.bfloat16)
-    cotangent = lax.all_gather(grad_out, "tp", axis=1, tiled=True)
+    peers = lax.axis_size("tp")
+    right = [(i, (i + 1) % peers) for i in range(peers)]
+    parts = [grad_out]
+    for stride in range(1, peers):
+        parts = [lax.ppermute(parts[0], "tp", right), *parts]
+    whole = jnp.concatenate(parts, axis=1)
+    shift = (lax.axis_index("tp") + 1) * parts[-1].shape[1]
+    cotangent = jnp.roll(whole, shift, axis=1)
     grad_normed = lax.dot_general(
         cotangent,
         lax.all_gather(out_weight, "seq", axis=1, tiled=True),

time: 687 us -> 639 us (0.930)
  waiting for transfers between devices: 471 us -> 415 us
  local copies, waits for them, and re-layouts: 46.9 us -> 55 us
    all_gather x1 -> x0, waiting for transfers between devices: 33 us -> none  [on_device(): cotangent = lax.all_gather(grad_out, 'tp', axis=1, tiled=True)]
    all_gather x2, waiting for transfers between devices: 32.6 us -> 0.01 us  [carried_in(): pieces = jax.tree.map(lambda part: lax.all_gather(part, axis), value)]
    ppermute x0 -> x3, waiting for transfers between devices: none -> 26.6 us  [on_device(): parts = [lax.ppermute(parts[0], 'tp', right), *parts]]
    all_gather x1, waiting for transfers between devices: 178 us -> 161 us  [on_device(): lax.all_gather(out_weight, 'seq', axis=1, tiled=True)]
    unnamed x46 -> x54, local copies, waits for them, and re-layouts: 19.6 us -> 22.9 us
  transfers between devices with their start and end apart: 6 -> 8, of which waited for: 5 -> 5; matrix products, arithmetic and copies ran while one was open for 16% -> 18% of each run, Pallas kernels for 0% -> 0%
where the time goes in v1:
time: 639 us; the launch traced here: 630 us
  waiting for transfers between devices  415 us (65%)
  matrix products  92.7 us (15%)
  local copies, waits for them, and re-layouts  55 us (9%)
  other arithmetic  24.8 us (4%)
  blocking collectives  21.7 us (3%)
  between operations  14.5 us (2%)
    all_to_all x1, waiting for transfers between devices, on_device(): lax.all_to_all(cotangent, 'seq', split_axis=1, concat_axis=0, tiled=True)  193 us
    all_gather x1, waiting for transfers between devices, on_device(): lax.all_gather(out_weight, 'seq', axis=1, tiled=True)  161 us
    all_gather x1, waiting for transfers between devices, on_device(): lax.all_gather(normed, 'seq', axis=0, tiled=True)  33.6 us
    ppermute x3, waiting for transfers between devices, on_device(): parts = [lax.ppermute(parts[0], 'tp', right), *parts]  26.6 us
    unnamed x54, local copies, waits for them, and re-layouts  22.9 us
    all_gather x1, blocking collectives, carried_in(): pieces = jax.tree.map(lambda part: lax.all_gather(part, axis), value)  21.7 us
    select_n x14, other arithmetic, turn(): jnp.where(position < mine, new, old)  16.9 us
  transfers between devices with their start and end apart: 8, of which 5 were waited for; matrix products, arithmetic and copies ran while one was open for 18% of the time, Pallas kernels for 0%

profile of v1, /device:TPU:0, one launch (start us, length us, event | category | flops | bytes accessed | tf_op | source)
XLA Modules:
  0.0 629.7 jit_solution(6949188642259650296)
XLA Ops:
  14.5 2.7 fusion.22
  18.2 4.5 fusion.47
  24.7 20.2 %collective-permute-done = bf16[512,1536]{0,1:T(8,128)(2,1)} collective-permute-done((bf16[512,1536]{0,1:T(8,128)(2,1)S(1)}, bf16[512,1536]{0,1:T(8,128)(2,1)}, u32[]{:S(2)}, u32[]{:S(2)}) %collective-permute-start) | collective-permute-done | bytes 1572896 | tf_op jit(solution)/shard_map/ppermute | solution.py:91
  49.5 21.7 %all-gather.2 = f32[8,1,8]{2,1,0:T(1,128)S(1)} all-gather(f32[1,1,8]{2,1,0:T(1,128)S(1)} %get-tuple-element.258), channel_id=1, replica_groups=mesh['seq'=8,'tp'=4] {'seq'}, dimensions={0}, use_global_device_ids=true | all-gather | bytes 288 | tf_op jit(solution)/shard_map/all_gather | solution.py:13
  71.3 6.4 %fusion.49 = f32[8,128,128,2]{2,3,1,0:T(2,128)} fusion(f32[2,8,128,128]{3,2,1,0:T(8,128)} %copy-done.19, pred[2,2]{1,0:T(4,128)(4,1)S(1)} %iota_compare_fusion.2, f32[2,8]{0,1:T(8,128)S(1)} %copy.183, f32[2,8]{0,1:T(8,128)S(1)} %bitcast.169), kind=kOutput, calls=%fused_computation.65 | convolution fusion | flops 6291552 | bytes 2097284 | tf_op jit(solution)/shard_map/nmh,mhde->nhde/dot_general | solution.py:72
  79.7 5.0 fusion.6
  84.7 6.5 %collective-permute-done.2 = bf16[512,1536]{0,1:T(8,128)(2,1)S(1)} collective-permute-done((bf16[512,1536]{0,1:T(8,128)(2,1)}, bf16[512,1536]{0,1:T(8,128)(2,1)S(1)}, u32[]{:S(2)}, u32[]{:S(2)}) %collective-permute-start.2) | collective-permute-done | bytes 1572896 | tf_op jit(solution)/shard_map/ppermute | solution.py:91
  97.7 4.3 constant_dynamic-slice_fusion
  102.0 8.8 %while.28 = (s32[]{:T(128)}, f32[8,128,128]{2,1,0:T(8,128)S(1)}, s32[]{:T(128)}, f32[8,8]{1,0:T(8,128)S(1)}, f32[8,8,128,128]{3,2,1,0:T(8,128)}, /*index=5*/s32[]{:T(128)}, s32[]{:T(128)}) while((s32[]{:T(128)}, f32[8,128,128]{2,1,0:T(8,128)S(1)}, s32[]{:T(128)}, f32[8,8]{1,0:T(8,128)S(1)}, f32[8,8,128,128]{3,2,1,0:T(8,128)}, ...), condition=%wide.region_4.5_spmd.clone, body=%wide.region_3.4_spmd.clone.sunk | while | flops 524292 | bytes 1573065 | solution.py:25
  110.8 3.6 multiply_reduce_fusion.1
  114.4 161.2 %all-gather.8.cloned.1.call-done = bf16[1024,6144]{1,0:T(8,128)(2,1)} async-done(((bf16[1024,768]{1,0:T(8,128)(2,1)}), bf16[1024,6144]{1,0:T(8,128)(2,1)}) %all-gather.8.cloned.1.call-update) | async-done | bytes 12582928 | tf_op jit(solution)/shard_map/all_gather | solution.py:97
  275.7 11.5 %convolution_bitcast_fusion = f32[64,8,8,128]{3,1,2,0:T(8,128)S(1)} fusion(bf16[512,6144]{0,1:T(8,128)(2,1)} %constant_dynamic-slice_fusion, bf16[1024,6144]{1,0:T(8,128)(2,1)} %all-gather.8.cloned.1.call-done), kind=kOutput, calls=%fused_computation.49 | convolution fusion | flops 6442450944 | bytes 20971520 | tf_op jit(solution)/shard_map/dot_general | solution.py:95
  289.1 3.2 copy.189
  294.5 3.1 fusion.93
  300.8 4.4 fusion.43
  305.3 4.8 all-to-all-start
  312.6 2.5 copy.278
  315.2 192.9 %all-to-all-done = bf16[512,8,768]{0,2,1:T(8,128)(2,1)} async-done(((bf16[512,8,768]{0,2,1:T(8,128)(2,1)}), bf16[512,8,768]{0,2,1:T(8,128)(2,1)}, u32[]{:S(2)}, u32[]{:S(2)}) %all-to-all-start) | async-done | bytes 6291488 | tf_op jit(solution)/shard_map/all_to_all | solution.py:127
  508.2 8.7 %copy.212 = bf16[8,512,768]{2,1,0:T(8,128)(2,1)} copy(bf16[8,512,768]{1,2,0:T(8,128)(2,1)} %bitcast.34) | data formatting | bytes 12582912 | tf_op jit(solution)/shard_map/all_to_all | solution.py:127
  516.8 3.2 fusion.53
  520.1 3.7 fusion.10
  523.8 3.2 fusion.17
  527.0 2.9 copy.195
  529.9 2.6 copy.279
  532.4 6.3 %fusion.45 = f32[8,128,128,2]{2,3,1,0:T(2,128)} fusion(f32[2,8,128,128]{3,2,1,0:T(8,128)} %copy-done.17, pred[2,2]{1,0:T(4,128)(4,1)S(1)} %iota_compare_fusion.1, f32[2,8]{0,1:T(8,128)S(1)} %copy.183, f32[2,8]{0,1:T(8,128)S(1)} %copy.200), kind=kOutput, calls=%fused_computation.61 | convolution fusion | flops 6291552 | bytes 2097284 | tf_op jit(solution)/shard_map/nmh,mhde->nhde/dot_general | solution.py:115
  538.7 8.0 %fusion.8 = f32[2,8,256,128]{3,2,1,0:T(8,128)} fusion(bf16[2,256,8,128]{1,3,2,0:T(8,128)(2,1)S(1)} %copy-done.6, f32[2,8,256,256]{3,2,1,0:T(8,128)} %copy-done.16, f32[2,8,256]{2,1,0:T(8,128)S(1)} %add_bitcast_fusion.1, pred[256,256]{1,0:T(8,128)(4,1)S(1)} %iota_compare_fusion), kind=kOutput, calls=%fused_computation.11 | convolution fusion | flops 1614807040 | bytes 7421952 | tf_op jit(solution)/shard_map/nhts,nthd->nshd/dot_general | solution.py:119
  546.7 9.2 %fusion.4 = f32[2,8,128,256]{2,3,1,0:T(8,128)} fusion(f32[2,256,8,128]{1,3,2,0:T(8,128)S(1)} %get-tuple-element.255, f32[2,8,256,256]{3,2,1,0:T(8,128)S(1)} %copy-done.3, f32[2,8,256]{2,1,0:T(8,128)S(1)} %add_bitcast_fusion.1, pred[256,256]{1,0:T(8,128)(4,1)S(1)} %iota_compare_fusion), kind=kOutput, calls=%fused_computation.9 | convolution fusion | flops 1614807040 | bytes 8470528 | tf_op jit(solution)/shard_map/nhts,nthe->nshe/dot_general | solution.py:123
  555.9 4.8 rev.7
  560.7 8.6 %while.29 = (s32[]{:T(128)}, f32[8,128,128]{2,1,0:T(8,128)S(1)}, s32[]{:T(128)}, f32[8,8]{1,0:T(8,128)S(1)}, f32[8,8,128,128]{3,2,1,0:T(8,128)}, /*index=5*/s32[]{:T(128)}, s32[]{:T(128)}) while((s32[]{:T(128)}, f32[8,128,128]{2,1,0:T(8,128)S(1)}, s32[]{:T(128)}, f32[8,8]{1,0:T(8,128)S(1)}, f32[8,8,128,128]{3,2,1,0:T(8,128)}, ...), condition=%wide.region_8.9_spmd.clone, body=%wide.region_7.8_spmd.clone.sunk | while | flops 524292 | bytes 1573065 | solution.py:25
  569.4 3.0 fusion.15
  577.3 33.6 %all-gather.10.cloned.1.call-done = bf16[4096,1024]{1,0:T(8,128)(2,1)} async-done(((bf16[512,1024]{1,0:T(8,128)(2,1)}), bf16[4096,1024]{1,0:T(8,128)(2,1)}) %all-gather.10.cloned.1.call-update) | async-done | bytes 8388624 | tf_op jit(solution)/shard_map/all_gather | solution.py:130
  610.9 12.1 %fusion.95 = f32[768,1024]{1,0:T(8,128)} fusion(bf16[4096,768]{1,0:T(8,128)(2,1)} %bitcast.154, bf16[4096,1024]{1,0:T(8,128)(2,1)} %all-gather.10.cloned.1.call-done), kind=kOutput, calls=%fused_computation.135 | convolution fusion | flops 6442450944 | bytes 17825792 | tf_op jit(solution)/shard_map/dot_general | solution.py:128
  (131 shorter events, 55.2 us)
Async XLA Ops:
  7.2 94.8 %all-gather.12.cloned.1.call-start = ((), (), s32[]{:S(2)}) async-start(), calls=%async_computation.3 | async-start | bytes 4718592 | tf_op jit(solution)/shard_map/all_gather | solution.py:13
  11.6 1.9 copy-start.11
  13.5 1.0 copy-start.8
  13.5 10.0 %copy-start.18 = (bf16[512,1536]{1,0:T(8,128)(2,1)S(1)}, bf16[512,1536]{1,0:T(8,128)(2,1)}, u32[]{:S(2)}) copy-start(bf16[512,1536]{1,0:T(8,128)(2,1)} %param.15) | copy-start | bytes 4718596
  17.2 1.0 copy-start.19
  22.7 253.0 %all-gather.8.cloned.1.call-start = ((), (), s32[]{:S(2)}) async-start(), calls=%async_computation.1 | async-start | bytes 14155776 | tf_op jit(solution)/shard_map/all_gather | solution.py:97
  23.4 532.5 %all-gather.14.cloned.1.call-start = ((), (), s32[]{:S(2)}) async-start(), calls=%async_computation.4 | async-start | bytes 4718592 | tf_op jit(solution)/shard_map/all_gather | solution.py:13
  24.2 20.7 %collective-permute-start = (bf16[512,1536]{0,1:T(8,128)(2,1)S(1)}, bf16[512,1536]{0,1:T(8,128)(2,1)}, u32[]{:S(2)}, u32[]{:S(2)}) collective-permute-start(bf16[512,1536]{0,1:T(8,128)(2,1)S(1)} %copy.172), channel_id=1, source_target_pairs={{0,1},{1,2},{2,3},{3,0},{4,5},{5,6},{6,7},{7,4},{8,9},{9,10},{10,1... | collective-permute-start | bytes 4718600 | tf_op jit(solution)/shard_map/ppermute | solution.py:91
  44.9 26.3 %collective-permute-start.1 = (bf16[512,1536]{0,1:T(8,128)(2,1)}, bf16[512,1536]{0,1:T(8,128)(2,1)}, u32[]{:S(2)}, u32[]{:S(2)}) collective-permute-start(bf16[512,1536]{0,1:T(8,128)(2,1)} %collective-permute-done), channel_id=1, source_target_pairs={{0,1},{1,2},{2,3},{3,0},{4,5},{5,6},{6,7},{7,4},{8,9},{9,10},{10,1... | collective-permute-start | bytes 4718600 | tf_op jit(solution)/shard_map/ppermute | solution.py:91
  49.4 30.3 %copy-start.4 = (bf16[2,256,8,128]{1,3,2,0:T(8,128)(2,1)}, bf16[2,256,8,128]{1,3,2,0:T(8,128)(2,1)S(1)}, u32[]{:S(2)}) copy-start(bf16[2,256,8,128]{1,3,2,0:T(8,128)(2,1)S(1)} %copy.198) | copy-start | bytes 3145732
  71.2 20.1 %collective-permute-start.2 = (bf16[512,1536]{0,1:T(8,128)(2,1)}, bf16[512,1536]{0,1:T(8,128)(2,1)S(1)}, u32[]{:S(2)}, u32[]{:S(2)}) collective-permute-start(bf16[512,1536]{0,1:T(8,128)(2,1)} %collective-permute-done.1), channel_id=1, source_target_pairs={{0,1},{1,2},{2,3},{3,0},{4,5},{5,6},{6,7},{7,4},{8,9},{9,10},{10,1... | collective-permute-start | bytes 4718600 | tf_op jit(solution)/shard_map/ppermute | solution.py:91
  71.3 8.4 %copy-start.9 = (bf16[64,8,8,128]{3,2,1,0:T(8,128)(2,1)S(1)}, bf16[64,8,8,128]{3,2,1,0:T(8,128)(2,1)}, u32[]{:S(2)}) copy-start(bf16[64,8,8,128]{3,2,1,0:T(8,128)(2,1)} %copy-done.8) | copy-start | bytes 3145732
  79.7 5.1 copy-start.2
  114.4 177.8 %copy-start = (f32[2,256,8,128]{1,3,2,0:T(8,128)}, f32[2,256,8,128]{1,3,2,0:T(8,128)S(1)}, u32[]{:S(2)}) copy-start(f32[2,256,8,128]{1,3,2,0:T(8,128)S(1)} %get-tuple-element.260) | copy-start | bytes 6291460
  292.2 2.2 copy-start.1
  294.4 3.2 copy-start.5
  299.8 1.0 copy-start.17
  305.3 202.9 %all-to-all-start = ((bf16[512,8,768]{0,2,1:T(8,128)(2,1)}), bf16[512,8,768]{0,2,1:T(8,128)(2,1)}, u32[]{:S(2)}, u32[]{:S(2)}) async-start(bf16[512,8,768]{0,2,1:T(8,128)(2,1)} %bitcast.144), calls=%async_computation | async-start | bytes 12582912 | tf_op jit(solution)/shard_map/all_to_all | solution.py:127
  310.1 300.8 %all-gather.10.cloned.1.call-start = ((), (), s32[]{:S(2)}) async-start(), calls=%async_computation.2 | async-start | bytes 9437184 | tf_op jit(solution)/shard_map/all_gather | solution.py:130
  516.8 3.2 copy-start.12
  520.1 3.7 copy-start.16
  520.1 3.7 copy-start.14
  529.9 8.9 %copy-start.6 = (bf16[2,256,8,128]{1,3,2,0:T(8,128)(2,1)S(1)}, bf16[2,256,8,128]{1,3,2,0:T(8,128)(2,1)}, u32[]{:S(2)}) copy-start(bf16[2,256,8,128]{1,3,2,0:T(8,128)(2,1)} %copy-done.4) | copy-start | bytes 3145732
  538.7 8.0 %copy-start.3 = (f32[2,8,256,256]{3,2,1,0:T(8,128)S(1)}, f32[2,8,256,256]{3,2,1,0:T(8,128)}, u32[]{:S(2)}) copy-start(f32[2,8,256,256]{3,2,1,0:T(8,128)} %copy-done.2) | copy-start | bytes 12582916
  555.9 13.4 %copy-start.10 = (bf16[64,8,8,128]{3,2,1,0:T(8,128)(2,1)S(1)}, bf16[64,8,8,128]{3,2,1,0:T(8,128)(2,1)}, u32[]{:S(2)}) copy-start(bf16[64,8,8,128]{3,2,1,0:T(8,128)(2,1)} %copy-done.8) | copy-start | bytes 3145732
  560.7 8.6 %copy-start.7 = (f32[8,128,128,2]{2,3,1,0:T(2,128)S(1)}, f32[8,128,128,2]{2,3,1,0:T(2,128)}, u32[]{:S(2)}) copy-start(f32[8,128,128,2]{2,3,1,0:T(2,128)} %fusion.45) | copy-start | bytes 3145732
  569.3 3.7 copy-start.13
  569.3 3.7 copy-start.15
Sparse Core Ops, SparseCore 0:
  22.8 76.1 all-gather.11
  101.1 174.4 all-gather.7
  305.4 177.9 all-gather.13
  485.4 125.4 all-gather.9
